TPU v7x, 256 devices: a whole 4x4x8 slice. The times are simulated.
256 devices in a mesh: space: 32 (over z, x), sample: 8 (over y, core).
Axes of the slice: x: 4, y: 4, z: 8, core: 2. Of those that a mesh axis runs over, the one named last changes fastest.
Arguments:
- crops: bfloat16 [256, 16, 64, 1024], P('sample', None, 'space'), may hold values from -6 to 6
- first_kernel: bfloat16 [32, 16, 3, 3, 3], replicated, may hold values from -0.3125 to 0.3125
- second_kernel: bfloat16 [64, 32, 3, 3, 3], replicated, may hold values from -0.21875 to 0.21875
- out_grad: bfloat16 [256, 64, 16, 64], P(('sample', 'space')), may hold values from -0.03125 to 0.03125
Outputs:
- features_out: bfloat16 [256, 64, 16, 64], P(('sample', 'space'))
- first_grad: float32 [32, 16, 3, 3, 3], replicated
- second_grad: float32 [64, 32, 3, 3, 3], replicated
All inputs are finite; a program needn't handle non-finite values.
Results may differ from a plain program's by a relative error of at most 0.012.
Values may be sent and summed in bfloat16 or wider, within the bound.
A program may use at most 128 MiB of HBM per device.

v0:
```python
import jax
import jax.numpy as jnp
from jax import lax
from jax.sharding import PartitionSpec as P

HEIGHT = 8
WIDTH = 128


def forward_conv(field, kernel, depth_pad):
    return lax.conv_general_dilated(
        field,
        kernel,
        (2, 2, 2),
        (depth_pad, (1, 0), (1, 0)),
        dimension_numbers=("NCDHW", "OIDHW", "NCDHW"),
        preferred_element_type=jnp.float32,
    )


def kernel_grad(field, cotangent, depth_pad):
    return lax.conv_general_dilated(
        field,
        cotangent,
        (1, 1, 1),
        (depth_pad, (1, 0), (1, 0)),
        rhs_dilation=(2, 2, 2),
        dimension_numbers=("CNDHW", "IODHW", "CNDHW"),
        preferred_element_type=jnp.float32,
    )


def input_grad(cotangent, kernel):
    flipped = kernel[:, :, ::-1, ::-1, ::-1]
    return lax.conv_general_dilated(
        cotangent,
        flipped,
        (1, 1, 1),
        ((1, 2), (1, 2), (1, 2)),
        lhs_dilation=(2, 2, 2),
        dimension_numbers=("NCDHW", "IODHW", "NCDHW"),
        preferred_element_type=jnp.float32,
    )


def silu_slope(value):
    sigma = jax.nn.sigmoid(value)
    return sigma * (1.0 + value * (1.0 - sigma))


def body(crops, first_kernel, second_kernel, out_grad):
    local_samples, channels_in, planes, flat_cells = crops.shape
    whole_input = lax.all_to_all(crops, "space", split_axis=0, concat_axis=2, tiled=True)
    whole_input = whole_input.reshape(
        whole_input.shape[0], channels_in, whole_input.shape[2], HEIGHT, WIDTH
    )
    first_pre = forward_conv(whole_input, first_kernel, (1, 0))
    act_whole = jax.nn.silu(first_pre).astype(jnp.bfloat16)
    sample_count = act_whole.shape[0]
    second_pre = forward_conv(act_whole, second_kernel, (1, 0))
    features_out = second_pre.astype(jnp.bfloat16).reshape(out_grad.shape)
    cotangent = out_grad.reshape(
        sample_count, out_grad.shape[1], out_grad.shape[2], HEIGHT // 4, WIDTH // 4
    )
    second_grad = kernel_grad(act_whole, cotangent, (1, 0))
    act_grad = input_grad(cotangent, second_kernel).astype(jnp.bfloat16)
    pre_grad = (act_grad.astype(jnp.float32) * silu_slope(first_pre)).astype(jnp.bfloat16)
    first_grad = kernel_grad(whole_input, pre_grad, (1, 0))
    first_grad, second_grad = lax.psum((first_grad, second_grad), ("space", "sample"))
    return (features_out, first_grad, second_grad)


def solution(mesh):
    placed = (P("sample", None, "space", None), P(), P(), P(("sample", "space"), None, None, None))
    return jax.shard_map(
        body,
        mesh=mesh,
        in_specs=placed,
        out_specs=(P(("sample", "space"), None, None, None), P(), P()),
        check_vma=False,
    )
```

profile of v0, /device:TPU:1, one launch (start us, length us, event | category | flops | bytes accessed | tf_op | source)
XLA Modules:
  0.0 415.9 jit_solution(15933746394667295038)
XLA Ops:
  7.2 0.0 copy-start
  7.2 0.0 copy-start.6
  7.2 12.0 %all-to-all-start = ((bf16[32,16,2,1024]{3,2,1,0:T(2,128)(2,1)}), bf16[32,16,2,1024]{3,2,1,0:T(2,128)(2,1)S(1)}, u32[]{:S(2)}, u32[]{:S(2)}) async-start(bf16[32,16,2,1024]{3,2,1,0:T(2,128)(2,1)} %param.4), calls=%async_computation | async-start | bytes 4194304 | tf_op jit(solution)/shard_map/all_to_all | solution.py:53
  19.2 0.0 all-reduce.2.cloned.1.call-start
  19.3 1.2 copy.72
  20.5 0.2 copy.91
  20.7 0.1 pad.4.clone
  20.7 0.1 copy.75
  20.8 0.0 copy-done
  20.9 0.0 copy-done.6
  20.9 2.4 fusion.19
  23.3 5.4 %copy.76 = f32[32,4,8,10,32]{4,0,3,2,1:T(8,128)} copy(f32[32,4,8,10,32]{4,2,3,1,0:T(8,128)S(1)} %fusion.19) | data formatting | bytes 2621440 | tf_op jit(solution)/shard_map/convert_element_type | solution.py:67
  28.7 39.0 %all-to-all-done = bf16[32,16,2,1024]{3,2,1,0:T(2,128)(2,1)S(1)} async-done(((bf16[32,16,2,1024]{3,2,1,0:T(2,128)(2,1)}), bf16[32,16,2,1024]{3,2,1,0:T(2,128)(2,1)S(1)}, u32[]{:S(2)}, u32[]{:S(2)}) %all-to-all-start) | async-done | bytes 2097184 | tf_op jit(solution)/shard_map/all_to_all | solution.py:53
  67.7 0.7 copy.60
  68.4 0.6 copy.92
  69.0 5.3 %copy.90 = bf16[16,64,8,1,128]{1,2,4,0,3:T(8,128)(2,1)} copy(bf16[16,64,8,1,128]{4,2,0,1,3:T(8,128)(2,1)S(1)} %bitcast.48) | data formatting | bytes 4194304
  74.3 5.6 %pad.clone = bf16[16,64,8,1,144]{1,2,4,0,3:T(8,128)(2,1)} pad(bf16[16,64,8,1,128]{1,2,4,0,3:T(8,128)(2,1)} %copy.90, bf16[]{:T(256)} %constant.6), padding=0_0x0_0x0_0x0_0x1_15 | pad | bytes 4456450 | tf_op jit(solution)/shard_map/reshape | solution.py:54
  79.9 0.0 copy-start.7
  79.9 0.0 copy-start.8
  79.9 32.5 %copy.63 = bf16[16,64,8,1,8,18]{0,4,5,2,1,3:T(8,128)(2,1)} copy(bf16[16,64,8,1,8,18]{1,2,5,4,0,3:T(8,128)(2,1)} %bitcast.50) | data formatting | bytes 4718592 | tf_op jit(solution)/shard_map/conv_general_dilated | solution.py:11
  112.4 3.9 slice.9
  116.2 0.0 copy-done.7
  116.2 0.0 copy-done.8
  116.3 20.1 %broadcast_select_fusion = (bf16[32,4,8,9,32]{4,2,3,1,0:T(8,128)(2,1)}, bf16[32,4,8,9,32]{4,2,3,1,0:T(8,128)(2,1)}, f32[32,4,8,9,32]{4,2,3,1,0:T(8,128)}) fusion(pred[8,9]{0,1:T(8,128)(4,1)S(1)} %copy-done.7, bf16[32,16,3,3,3]{0,1,4,3,2:T(8,128)(2,1)S(1)} %copy-done.8, bf16[16,64,8,1,7,2]{0,4,5,2,1,3:T(8,128)(2,1)} %slice.9, ...), kind=kOutput, calls=%fused_computation.30 | convolution fusion | flops 241065984 | bytes 4975688 | tf_op jit(solution)/shard_map/conv_general_dilated | solution.py:11
  136.4 2.6 copy.64
  139.0 0.0 copy-start.3
  139.0 0.4 slice.10
  139.4 1.4 copy.66
  140.8 0.0 copy-start.1
  140.8 1.0 fusion.48
  141.8 0.4 copy-done.1
  142.3 0.0 copy-done.3
  142.3 0.9 copy.80
  143.2 1.7 slice.16
  144.9 12.4 %fusion.9 = f32[64,32,3,3,3]{0,1,4,3,2:T(8,128)} fusion(bf16[32,4,1,64,32]{4,0,3,1,2:T(8,128)(2,1)} %slice.16, bf16[1,64,16,2,32]{1,4,3,2,0:T(8,128)(2,1)S(1)} %bitcast.60), kind=kOutput, calls=%fused_computation.16 | convolution fusion | flops 91443200 | bytes 876544 | tf_op jit(solution)/shard_map/conv_general_dilated | solution.py:22
  157.3 0.0 all-reduce.2.cloned.1.call-update
  157.3 3.9 add_multiply_fusion
  161.2 4.9 %copy.77 = f32[32,4,8,9,32]{4,0,3,2,1:T(8,128)} copy(f32[32,4,8,9,32]{4,2,3,1,0:T(8,128)S(1)} %add_multiply_fusion) | data formatting | bytes 2359296 | tf_op jit(solution)/shard_map/mul | solution.py:48
  166.1 35.1 %copy.78 = bf16[1,16,64,8,128]{1,0,4,3,2:T(2,128)(2,1)} copy(bf16[1,16,64,8,128]{4,3,1,2,0:T(8,128)(2,1)S(1)} %bitcast.49) | data formatting | bytes 4194304 | tf_op jit(solution)/shard_map/reshape | solution.py:54
  201.2 4.5 %fusion.8 = bf16[32,4,1,64,32]{4,0,3,1,2:T(8,128)(2,1)S(1)} fusion(f32[32,4,1,72,32]{4,0,3,1,2:T(8,128)} %bitcast.52, f32[32,4,1,80,32]{4,0,3,1,2:T(8,128)} %bitcast.51), kind=kLoop, calls=%fused_computation.15 | loop fusion | flops 524288 | bytes 2621440 | tf_op jit(solution)/shard_map/convert_element_type | solution.py:67
  205.7 0.0 copy-start.2
  205.7 0.0 copy-start.4
  205.7 0.0 copy-start.5
  205.7 89.5 %fusion.11 = f32[32,16,3,3,3]{0,1,4,3,2:T(8,128)S(1)} fusion(bf16[1,16,64,8,128]{1,0,4,3,2:T(2,128)(2,1)} %copy.78, bf16[32,4,1,64,32]{4,0,3,1,2:T(8,128)(2,1)S(1)} %fusion.8), kind=kOutput, calls=%fused_computation.18 | convolution fusion | flops 204385280 | bytes 2676736 | tf_op jit(solution)/shard_map/conv_general_dilated | solution.py:22
  295.2 0.0 copy-done.2
  295.3 0.0 copy-done.4
  295.3 0.0 copy-done.5
  295.3 1.8 fusion.26
  297.1 0.2 copy.69
  297.3 1.1 copy.84
  298.4 79.8 %psum.14 = f32[32,16,3,3,3]{0,1,4,3,2:T(8,128)} all-reduce(f32[32,16,3,3,3]{0,1,4,3,2:T(8,128)S(1)} %fusion.11), channel_id=1, replica_groups=mesh['space'=32,'sample'=8] {'space','sample'}, use_global_device_ids=true, to_apply=%region_0.1 | all-reduce | flops 13824 | bytes 110592 | tf_op jit(solution)/shard_map/psum | solution.py:69
  378.2 28.8 %all-reduce.2.cloned.1.call-done = f32[64,32,3,3,3]{0,1,4,3,2:T(8,128)} async-done(((f32[64,32,3,3,3]{0,1,4,3,2:T(8,128)}), f32[64,32,3,3,3]{0,1,4,3,2:T(8,128)}) %all-reduce.2.cloned.1.call-update) | async-done | bytes 221200 | tf_op jit(solution)/shard_map/psum | solution.py:69
  407.0 1.8 copy.101
  (1 shorter events, 0.0 us)
Async XLA Ops:
  7.2 13.7 %copy-start = (bf16[64,32,3,3,3]{0,1,4,3,2:T(8,128)(2,1)S(1)}, bf16[64,32,3,3,3]{0,1,4,3,2:T(8,128)(2,1)}, u32[]{:S(2)}) copy-start(bf16[64,32,3,3,3]{0,1,4,3,2:T(8,128)(2,1)} %param.6) | copy-start | bytes 331780
  7.2 13.7 %copy-start.6 = (pred[8,10]{0,1:T(8,128)(4,1)S(1)}, pred[8,10]{0,1:T(8,128)(4,1)}, u32[]{:S(2)}) copy-start(pred[8,10]{0,1:T(8,128)(4,1)} %constant.19) | copy-start | bytes 244
  7.2 60.5 %all-to-all-start = ((bf16[32,16,2,1024]{3,2,1,0:T(2,128)(2,1)}), bf16[32,16,2,1024]{3,2,1,0:T(2,128)(2,1)S(1)}, u32[]{:S(2)}, u32[]{:S(2)}) async-start(bf16[32,16,2,1024]{3,2,1,0:T(2,128)(2,1)} %param.4), calls=%async_computation | async-start | bytes 4194304 | tf_op jit(solution)/shard_map/all_to_all | solution.py:53
  19.2 387.8 %all-reduce.2.cloned.1.call-start = ((), (), s32[]{:S(2)}) async-start(), calls=%async_computation.1 | async-start | bytes 884736 | tf_op jit(solution)/shard_map/psum | solution.py:69
  79.9 36.3 %copy-start.7 = (pred[8,9]{0,1:T(8,128)(4,1)S(1)}, pred[8,9]{0,1:T(8,128)(4,1)}, u32[]{:S(2)}) copy-start(pred[8,9]{0,1:T(8,128)(4,1)} %constant.17) | copy-start | bytes 220
  79.9 36.3 %copy-start.8 = (bf16[32,16,3,3,3]{0,1,4,3,2:T(8,128)(2,1)S(1)}, bf16[32,16,3,3,3]{0,1,4,3,2:T(8,128)(2,1)}, u32[]{:S(2)}) copy-start(bf16[32,16,3,3,3]{0,1,4,3,2:T(8,128)(2,1)} %param.5) | copy-start | bytes 82948
  139.0 3.3 copy-start.3
  140.8 1.5 copy-start.1
  205.7 89.6 %copy-start.2 = (bf16[32,4,1,8,8,32]{5,3,4,1,0,2:T(8,128)(2,1)S(1)}, bf16[32,4,1,8,8,32]{5,3,4,1,0,2:T(8,128)(2,1)}, u32[]{:S(2)}) copy-start(bf16[32,4,1,8,8,32]{5,3,4,1,0,2:T(8,128)(2,1)} %copy-done.1) | copy-start | bytes 1572868
  205.7 89.6 %copy-start.4 = (bf16[32,4,1,7,1,32]{5,3,4,1,0,2:T(8,128)(2,1)S(1)}, bf16[32,4,1,7,1,32]{5,3,4,1,0,2:T(8,128)(2,1)}, u32[]{:S(2)}) copy-start(bf16[32,4,1,7,1,32]{5,3,4,1,0,2:T(8,128)(2,1)} %get-tuple-element.14) | copy-start | bytes 172036
  205.7 89.6 %copy-start.5 = (bf16[32,4,1,7,1,32]{5,3,4,1,0,2:T(8,128)(2,1)S(1)}, bf16[32,4,1,7,1,32]{5,3,4,1,0,2:T(8,128)(2,1)}, u32[]{:S(2)}) copy-start(bf16[32,4,1,7,1,32]{5,3,4,1,0,2:T(8,128)(2,1)} %get-tuple-element.15) | copy-start | bytes 172036
Sparse Core Ops, SparseCore 0:
  157.4 249.5 all-reduce.1
where the time goes:
time: 422 us; the launch traced here: 416 us
  matrix products  126 us (30%)
  local copies, waits for them, and re-layouts  107 us (25%)
  blocking collectives  79.8 us (19%)
  waiting for transfers between devices  67.7 us (16%)
  between operations  14.5 us (3%)
  starting transfers between devices  12 us (3%)
  other arithmetic  8.48 us (2%)
    conv_general_dilated x2, matrix products, kernel_grad(): lax.conv_general_dilated(field, cotangent, (1, 1, 1), (depth_pad, (1, 0),...  102 us
    psum x1, blocking collectives, body(): lax.psum((first_grad, second_grad), ('space', 'sample'))  79.8 us
    reshape x2, local copies, waits for them, and re-layouts, body(): whole_input.reshape(whole_input.shape[0], channels_in, whole_input.shape[...  40.7 us
    all_to_all x1, waiting for transfers between devices, body(): lax.all_to_all(crops, 'space', split_axis=0, concat_axis=2, tiled=True)  39 us
    conv_general_dilated x2, local copies, waits for them, and re-layouts, forward_conv(): lax.conv_general_dilated(field, kernel, (2, 2, 2), (depth_pad, (1, 0), (1...  36.3 us
    psum x1, waiting for transfers between devices, body(): lax.psum((first_grad, second_grad), ('space', 'sample'))  28.8 us
    conv_general_dilated x2, matrix products, forward_conv(): lax.conv_general_dilated(field, kernel, (2, 2, 2), (depth_pad, (1, 0), (1...  22 us
    all_to_all x1, starting transfers between devices, body(): lax.all_to_all(crops, 'space', split_axis=0, concat_axis=2, tiled=True)  12 us
  transfers between devices with their start and end apart: 2, of which 2 were waited for; matrix products, arithmetic and copies ran while one was open for 36% of the time, Pallas kernels for 0%

commit v1 on v0

--- a/solution.py
+++ b/solution.py
@@ -66,7 +66,7 @@
     act_grad = input_grad(cotangent, second_kernel).astype(jnp.bfloat16)
     pre_grad = (act_grad.astype(jnp.float32) * silu_slope(first_pre)).astype(jnp.bfloat16)
     first_grad = kernel_grad(whole_input, pre_grad, (1, 0))
-    first_grad, second_grad = lax.psum((first_grad, second_grad), ("space", "sample"))
+    first_grad, second_grad = lax.psum(lax.psum((first_grad, second_grad), "sample"), "space")
     return (features_out, first_grad, second_grad)
 
 

time: 422 us -> 480 us (1.14)
  the two profiles are of different devices: /device:TPU:1 before, /device:TPU:0 now
where the time goes in v1:
time: 480 us; the launch traced here: 473 us
  blocking collectives  169 us (35%)
  matrix products  125 us (26%)
  local copies, waits for them, and re-layouts  105 us (22%)
  waiting for transfers between devices  40.7 us (8%)
  between operations  14.5 us (3%)
  starting transfers between devices  9.81 us (2%)
  other arithmetic  8.46 us (2%)
    psum x1, blocking collectives, body(): lax.psum(lax.psum((first_grad, second_grad), 'sample'), 'space')  143 us
    conv_general_dilated x2, matrix products, kernel_grad(): lax.conv_general_dilated(field, cotangent, (1, 1, 1), (depth_pad, (1, 0),...  101 us
    all_to_all x1, waiting for transfers between devices, body(): lax.all_to_all(crops, 'space', split_axis=0, concat_axis=2, tiled=True)  40.6 us
    reshape x2, local copies, waits for them, and re-layouts, body(): whole_input.reshape(whole_input.shape[0], channels_in, whole_input.shape[...  40.4 us
    conv_general_dilated x2, local copies, waits for them, and re-layouts, forward_conv(): lax.conv_general_dilated(field, kernel, (2, 2, 2), (depth_pad, (1, 0), (1...  36.3 us
    psum x1, blocking collectives, body(): lax.psum((first_grad, second_grad), 'sample')  26.4 us
    conv_general_dilated x2, matrix products, forward_conv(): lax.conv_general_dilated(field, kernel, (2, 2, 2), (depth_pad, (1, 0), (1...  22 us
    unnamed x18, local copies, waits for them, and re-layouts  10.2 us
  transfers between devices with their start and end apart: 3, of which 1 were waited for; matrix products, arithmetic and copies ran while one was open for 32% of the time, Pallas kernels for 0%

profile of v1, /device:TPU:0, one launch (start us, length us, event | category | flops | bytes accessed | tf_op | source)
XLA Modules:
  0.0 473.4 jit_solution(460807770984108524)
XLA Ops:
  7.2 0.0 copy-start
  7.2 0.0 copy-start.3
  7.2 9.7 %all-to-all-start = ((bf16[32,16,2,1024]{3,2,1,0:T(2,128)(2,1)}), bf16[32,16,2,1024]{3,2,1,0:T(2,128)(2,1)S(1)}, u32[]{:S(2)}, u32[]{:S(2)}) async-start(bf16[32,16,2,1024]{3,2,1,0:T(2,128)(2,1)} %param.4), calls=%async_computation | async-start | bytes 4194304 | tf_op jit(solution)/shard_map/all_to_all | solution.py:53
  16.9 0.0 all-reduce.3.cloned.1.call-start
  17.0 1.2 copy.72
  18.2 0.2 copy.91
  18.4 0.1 pad.4.clone
  18.4 0.1 copy.75
  18.6 0.0 copy-done
  18.6 0.0 copy-done.3
  18.6 2.4 fusion.19
  21.0 5.4 %copy.76 = f32[32,4,8,10,32]{4,0,3,2,1:T(8,128)} copy(f32[32,4,8,10,32]{4,2,3,1,0:T(8,128)S(1)} %fusion.19) | data formatting | bytes 2621440 | tf_op jit(solution)/shard_map/convert_element_type | solution.py:67
  26.4 40.6 %all-to-all-done = bf16[32,16,2,1024]{3,2,1,0:T(2,128)(2,1)S(1)} async-done(((bf16[32,16,2,1024]{3,2,1,0:T(2,128)(2,1)}), bf16[32,16,2,1024]{3,2,1,0:T(2,128)(2,1)S(1)}, u32[]{:S(2)}, u32[]{:S(2)}) %all-to-all-start) | async-done | bytes 2097184 | tf_op jit(solution)/shard_map/all_to_all | solution.py:53
  67.1 0.7 copy.60
  67.8 0.6 copy.92
  68.4 5.3 %copy.90 = bf16[16,64,8,1,128]{1,2,4,0,3:T(8,128)(2,1)} copy(bf16[16,64,8,1,128]{4,2,0,1,3:T(8,128)(2,1)S(1)} %bitcast.48) | data formatting | bytes 4194304
  73.7 5.6 %pad.clone = bf16[16,64,8,1,144]{1,2,4,0,3:T(8,128)(2,1)} pad(bf16[16,64,8,1,128]{1,2,4,0,3:T(8,128)(2,1)} %copy.90, bf16[]{:T(256)} %constant.6), padding=0_0x0_0x0_0x0_0x1_15 | pad | bytes 4456450 | tf_op jit(solution)/shard_map/reshape | solution.py:54
  79.3 0.0 copy-start.4
  79.3 0.0 copy-start.5
  79.3 32.5 %copy.63 = bf16[16,64,8,1,8,18]{0,4,5,2,1,3:T(8,128)(2,1)} copy(bf16[16,64,8,1,8,18]{1,2,5,4,0,3:T(8,128)(2,1)} %bitcast.50) | data formatting | bytes 4718592 | tf_op jit(solution)/shard_map/conv_general_dilated | solution.py:11
  111.7 3.8 slice.9
  115.6 0.0 copy-done.4
  115.6 0.0 copy-done.5
  115.6 20.2 %broadcast_select_fusion = (bf16[32,4,8,9,32]{4,2,3,1,0:T(8,128)(2,1)}, bf16[32,4,8,9,32]{4,2,3,1,0:T(8,128)(2,1)}, f32[32,4,8,9,32]{4,2,3,1,0:T(8,128)}) fusion(pred[8,9]{0,1:T(8,128)(4,1)S(1)} %copy-done.4, bf16[32,16,3,3,3]{0,1,4,3,2:T(8,128)(2,1)S(1)} %copy-done.5, bf16[16,64,8,1,7,2]{0,4,5,2,1,3:T(8,128)(2,1)} %slice.9, ...), kind=kOutput, calls=%fused_computation.30 | convolution fusion | flops 241065984 | bytes 4975688 | tf_op jit(solution)/shard_map/conv_general_dilated | solution.py:11
  135.7 2.6 copy.64
  138.3 0.0 copy-start.2
  138.3 0.4 slice.10
  138.8 2.6 copy.66
  141.4 0.0 copy-done.2
  141.4 0.9 copy.80
  142.3 0.4 slice.16
  142.7 11.8 %fusion.9 = f32[64,32,3,3,3]{0,1,4,3,2:T(8,128)} fusion(bf16[32,4,1,64,32]{4,0,3,1,2:T(8,128)(2,1)S(1)} %slice.16, bf16[1,64,16,2,32]{1,4,3,2,0:T(8,128)(2,1)S(1)} %bitcast.60), kind=kOutput, calls=%fused_computation.16 | convolution fusion | flops 91443200 | bytes 876544 | tf_op jit(solution)/shard_map/conv_general_dilated | solution.py:22
  154.5 0.0 all-reduce.3.cloned.1.call-update
  154.5 0.0 all-reduce.5.cloned.1.call-start
  154.6 3.9 add_multiply_fusion
  158.5 4.9 %copy.77 = f32[32,4,8,9,32]{4,0,3,2,1:T(8,128)} copy(f32[32,4,8,9,32]{4,2,3,1,0:T(8,128)S(1)} %add_multiply_fusion) | data formatting | bytes 2359296 | tf_op jit(solution)/shard_map/mul | solution.py:48
  163.4 34.8 %copy.78 = bf16[1,16,64,8,128]{1,0,4,3,2:T(2,128)(2,1)} copy(bf16[1,16,64,8,128]{4,3,1,2,0:T(8,128)(2,1)S(1)} %bitcast.49) | data formatting | bytes 4194304 | tf_op jit(solution)/shard_map/reshape | solution.py:54
  198.2 4.5 fusion.8
  202.7 0.0 copy-start.1
  202.8 89.3 %fusion.11 = f32[32,16,3,3,3]{0,1,4,3,2:T(8,128)S(1)} fusion(bf16[1,16,64,8,128]{1,0,4,3,2:T(2,128)(2,1)} %copy.78, bf16[32,4,1,64,32]{4,0,3,1,2:T(8,128)(2,1)S(1)} %fusion.8), kind=kOutput, calls=%fused_computation.18 | convolution fusion | flops 204385280 | bytes 2676736 | tf_op jit(solution)/shard_map/conv_general_dilated | solution.py:22
  292.0 0.0 copy-done.1
  292.0 0.1 fusion.48
  292.1 0.0 all-reduce.3.cloned.1.call-done
  292.2 0.0 all-reduce.5.cloned.1.call-update
  292.2 1.8 fusion.26
  294.0 0.2 copy.69
  294.2 1.1 copy.84
  295.3 26.4 %psum.28 = f32[32,16,3,3,3]{0,1,4,3,2:T(8,128)S(1)} all-reduce(f32[32,16,3,3,3]{0,1,4,3,2:T(8,128)S(1)} %fusion.11), channel_id=1, replica_groups=mesh['space'=32,'sample'=8] {'sample'}, use_global_device_ids=true, to_apply=%region_0.1 | all-reduce | flops 13824 | bytes 110592 | tf_op jit(solution)/shard_map/psum | solution.py:69
  321.7 142.8 %psum.29 = f32[32,16,3,3,3]{0,1,4,3,2:T(8,128)} all-reduce(f32[32,16,3,3,3]{0,1,4,3,2:T(8,128)S(1)} %psum.28), channel_id=1, replica_groups=mesh['space'=32,'sample'=8] {'space'}, use_global_device_ids=true, to_apply=%region_1.2 | all-reduce | flops 13824 | bytes 110592 | tf_op jit(solution)/shard_map/psum | solution.py:69
  464.6 0.0 all-reduce.5.cloned.1.call-done
  464.6 1.8 copy.102
  (1 shorter events, 0.0 us)
Async XLA Ops:
  7.2 11.4 %copy-start = (bf16[64,32,3,3,3]{0,1,4,3,2:T(8,128)(2,1)S(1)}, bf16[64,32,3,3,3]{0,1,4,3,2:T(8,128)(2,1)}, u32[]{:S(2)}) copy-start(bf16[64,32,3,3,3]{0,1,4,3,2:T(8,128)(2,1)} %param.6) | copy-start | bytes 331780
  7.2 11.4 %copy-start.3 = (pred[8,10]{0,1:T(8,128)(4,1)S(1)}, pred[8,10]{0,1:T(8,128)(4,1)}, u32[]{:S(2)}) copy-start(pred[8,10]{0,1:T(8,128)(4,1)} %constant.19) | copy-start | bytes 244
  7.2 59.9 %all-to-all-start = ((bf16[32,16,2,1024]{3,2,1,0:T(2,128)(2,1)}), bf16[32,16,2,1024]{3,2,1,0:T(2,128)(2,1)S(1)}, u32[]{:S(2)}, u32[]{:S(2)}) async-start(bf16[32,16,2,1024]{3,2,1,0:T(2,128)(2,1)} %param.4), calls=%async_computation | async-start | bytes 4194304 | tf_op jit(solution)/shard_map/all_to_all | solution.py:53
  16.9 275.2 %all-reduce.3.cloned.1.call-start = ((), (), s32[]{:S(2)}) async-start(), calls=%async_computation.1 | async-start | bytes 884736 | tf_op jit(solution)/shard_map/psum | solution.py:69
  79.3 36.3 %copy-start.4 = (pred[8,9]{0,1:T(8,128)(4,1)S(1)}, pred[8,9]{0,1:T(8,128)(4,1)}, u32[]{:S(2)}) copy-start(pred[8,9]{0,1:T(8,128)(4,1)} %constant.17) | copy-start | bytes 220
  79.3 36.3 %copy-start.5 = (bf16[32,16,3,3,3]{0,1,4,3,2:T(8,128)(2,1)S(1)}, bf16[32,16,3,3,3]{0,1,4,3,2:T(8,128)(2,1)}, u32[]{:S(2)}) copy-start(bf16[32,16,3,3,3]{0,1,4,3,2:T(8,128)(2,1)} %param.5) | copy-start | bytes 82948
  138.3 3.1 copy-start.2
  154.5 310.0 %all-reduce.5.cloned.1.call-start = ((), (), s32[]{:S(2)}) async-start(), calls=%async_computation.2 | async-start | bytes 884736 | tf_op jit(solution)/shard_map/psum | solution.py:69
  202.7 89.3 %copy-start.1 = (bf16[32,4,1,8,8,32]{5,3,4,1,0,2:T(8,128)(2,1)S(1)}, bf16[32,4,1,8,8,32]{5,3,4,1,0,2:T(8,128)(2,1)}, u32[]{:S(2)}) copy-start(bf16[32,4,1,8,8,32]{5,3,4,1,0,2:T(8,128)(2,1)} %copy.66) | copy-start | bytes 1572868
Sparse Core Ops, SparseCore 0:
  154.7 63.2 all-reduce.2
  292.3 144.7 all-reduce.4
